TPU v7x, 32 devices: a whole 2x2x4 slice. The times are simulated.
32 devices in a mesh: rows: 8 (over z, y), rhs: 4 (over x, core).
Axes of the slice: x: 2, y: 2, z: 4, core: 2. Of those that a mesh axis runs over, the one named last changes fastest.
Arguments:
- right_sides: bfloat16 [65536, 1024], P(None, ('rows', 'rhs')), may hold values from -6 to 6
- col_panels: bfloat16 [2, 65536, 1024], P(None, ('rows', 'rhs')), may hold values from -0.1875 to 0.1875
- diag_inverses: bfloat16 [2, 1024, 1024], replicated, may hold values from -0.1875 to 0.1875
Outputs:
- current: float32 [65536, 1024], P(('rows', 'rhs'))
All inputs are finite; a program needn't handle non-finite values.
Results may differ from a plain program's by a relative error of at most 0.003.
Values may be sent and summed in bfloat16 or wider, within the bound.
No kernel may reach another device: no remote copies, remote signals or barrier semaphores. Data moves between devices by JAX's collectives and lax.ppermute only.
A program may use at most 128 MiB of HBM per device.

v0:
```python
import jax
import jax.numpy as jnp
from jax import lax
from jax.sharding import PartitionSpec as P


def spread(shard, axis, root):
    mine = lax.axis_index(axis) == root
    return lax.psum(jnp.where(mine, shard, jnp.zeros_like(shard)), axis)


def local(right_sides, col_panels, diag_inverses):
    panel_size = diag_inverses.shape[1]
    early_solved = None
    gathered = lax.all_to_all(right_sides, ("rows", "rhs"), split_axis=0, concat_axis=1, tiled=True)
    current = gathered.astype(jnp.float32)
    rows_dev = current.shape[0]
    panel_count = diag_inverses.shape[0]
    devices_all = lax.axis_size("rows") * lax.axis_size("rhs")
    position = lax.axis_index(("rows", "rhs"))
    global_rows = position * rows_dev + jnp.arange(rows_dev, dtype=jnp.int32)
    for panel_id in range(panel_count):
        owner_dev = panel_id * devices_all // panel_count
        first_row = owner_dev * rows_dev
        is_owner = position == owner_dev
        local_panel = current[:panel_size].astype(jnp.bfloat16)
        inverse_now = diag_inverses[panel_id]
        solved_here = lax.cond(
            is_owner,
            lambda: jnp.dot(inverse_now, local_panel, preferred_element_type=jnp.float32).astype(
                jnp.bfloat16
            ),
            lambda: jnp.zeros(local_panel.shape, jnp.bfloat16),
        )
        solved = spread(solved_here, ("rows", "rhs"), owner_dev)
        update_term = jnp.dot(col_panels[panel_id], solved, preferred_element_type=jnp.float32)
        trailing = (global_rows >= first_row + panel_size)[:, None]
        current = jnp.where(trailing, current - update_term, current)
        top_rows = jnp.where(is_owner, solved.astype(jnp.float32), current[:panel_size])
        current = jnp.concatenate([top_rows, current[panel_size:]], axis=0)
    return current


def solution(mesh):
    return jax.shard_map(
        local,
        mesh=mesh,
        in_specs=(P(None, ("rows", "rhs")), P(None, ("rows", "rhs"), None), P()),
        out_specs=P(("rows", "rhs"), None),
        check_vma=False,
    )
```

profile of v0, /device:TPU:0, one launch (start us, length us, event | category | flops | bytes accessed | tf_op | source)
XLA Modules:
  0.0 446.5 jit_solution(2553022597957633385)
XLA Ops:
  6.5 4.8 %copy.27 = bf16[4,32,8,2048]{3,2,0,1:T(8,128)(2,1)} copy(bf16[4,32,8,2048]{3,2,1,0:T(8,128)(2,1)} %bitcast.34) | data formatting | bytes 8388608 | tf_op jit(solution)/shard_map/all_to_all | solution.py:15
  11.3 7.4 %all-to-all-start = ((bf16[32,2048,32]{1,2,0:T(8,128)(2,1)}), bf16[32,2048,32]{1,2,0:T(8,128)(2,1)}, u32[]{:S(2)}, u32[]{:S(2)}) async-start(bf16[32,2048,32]{1,2,0:T(8,128)(2,1)} %bitcast.33), calls=%async_computation | async-start | bytes 8388608 | tf_op jit(solution)/shard_map/all_to_all | solution.py:15
  18.8 0.0 all-reduce.3.cloned.1.call-start
  18.8 93.8 %all-to-all-done = bf16[32,2048,32]{1,2,0:T(8,128)(2,1)} async-done(((bf16[32,2048,32]{1,2,0:T(8,128)(2,1)}), bf16[32,2048,32]{1,2,0:T(8,128)(2,1)}, u32[]{:S(2)}, u32[]{:S(2)}) %all-to-all-start) | async-done | bytes 4194336 | tf_op jit(solution)/shard_map/all_to_all | solution.py:15
  112.6 9.4 %conditional.2 = (bf16[1024,1024]{0,1:T(8,128)(2,1)S(1)}) conditional(s32[]{:T(128)} %convert_element_type.35, () %tuple.18, (bf16[2,1024,1024]{2,1,0:T(8,128)(2,1)}, bf16[2048,32,32]{0,2,1:T(8,128)(2,1)}) %tuple.19), branch_computations={%region_0.0_spmd, %region_1.0_spmd} | conditional | flops 2148532224 | bytes 31457316 | solution.py:28
  112.6 0.0 copy-start.2
  112.6 2.0 slice.38
  114.6 0.9 copy-done.2
  115.4 3.7 fusion.3
  119.1 2.9 copy.22
  122.0 1.5 broadcast_select_fusion
  123.5 0.0 all-reduce.3.cloned.1.call-update
  123.5 0.0 all-reduce.5.cloned.1.call-start
  123.6 129.8 %all-reduce.3.cloned.1.call-done = bf16[1024,1024]{0,1:T(8,128)(2,1)} async-done(((bf16[1024,1024]{0,1:T(8,128)(2,1)}), bf16[1024,1024]{0,1:T(8,128)(2,1)}) %all-reduce.3.cloned.1.call-update) | async-done | bytes 2097168 | tf_op jit(solution)/shard_map/psum | solution.py:9
  253.3 0.0 copy-start
  253.3 8.7 %subtract_select_fusion.1 = f32[2048,1024]{0,1:T(8,128)S(1)} fusion(bf16[2048,1024]{0,1:T(8,128)(2,1)} %bitcast.9, bf16[1024,1024]{0,1:T(8,128)(2,1)} %all-reduce.3.cloned.1.call-done, bf16[2,2048,1024]{2,1,0:T(8,128)(2,1)} %param.8, pred[2048]{0:T(1024)(128)(4,1)S(1)} %fusion.17), kind=kOutput, calls=%fused_computation.9 | convolution fusion | flops 4301258752 | bytes 18876416 | tf_op jit(solution)/shard_map/dot_general | solution.py:36
  262.1 0.0 copy-done
  262.1 4.9 %fusion.18 = (bf16[1024,1024]{0,1:T(8,128)(2,1)}, f32[1024,1024]{0,1:T(8,128)}, f32[1024,1024]{0,1:T(8,128)}) fusion(f32[2048,1024]{0,1:T(8,128)S(1)} %subtract_select_fusion.1, bf16[1024,1024]{0,1:T(8,128)(2,1)S(1)} %copy-done, pred[]{:T(512)S(6)} %eq.9), kind=kLoop, calls=%fused_computation.23 | loop fusion | flops 3145728 | bytes 20971520 | tf_op jit(solution)/shard_map/convert_element_type | solution.py:26
  266.9 0.4 conditional.3
  266.9 0.3 broadcast.22.clone
  267.4 1.5 broadcast_select_fusion.1
  268.9 0.0 all-reduce.5.cloned.1.call-update
  268.9 139.6 %all-reduce.5.cloned.1.call-done = bf16[1024,1024]{0,1:T(8,128)(2,1)} async-done(((bf16[1024,1024]{0,1:T(8,128)(2,1)}), bf16[1024,1024]{0,1:T(8,128)(2,1)}) %all-reduce.5.cloned.1.call-update) | async-done | bytes 2097168 | tf_op jit(solution)/shard_map/psum | solution.py:9
  408.5 0.0 copy-start.1
  408.5 13.3 %subtract_select_fusion = f32[2048,1024]{0,1:T(8,128)} fusion(f32[1024,1024]{0,1:T(8,128)} %get-tuple-element.43, f32[1024,1024]{0,1:T(8,128)} %get-tuple-element.40, bf16[1024,1024]{0,1:T(8,128)(2,1)} %all-reduce.5.cloned.1.call-done, bf16[2,2048,1024]{2,1,0:T(8,128)(2,1)} %param.8, pred[2048]{0:T(1024)(128)(4,1)S(1)} %fusion.16), kind=kOutput, calls=%fused_computation.8 | convolution fusion | flops 4301258752 | bytes 23070720 | tf_op jit(solution)/shard_map/dot_general | solution.py:36
  421.9 0.0 copy-done.1
  421.9 4.7 %slice_select_fusion = (f32[1024,1024]{0,1:T(8,128)S(1)}, f32[1024,1024]{0,1:T(8,128)S(1)}) fusion(f32[2048,1024]{0,1:T(8,128)} %subtract_select_fusion, bf16[1024,1024]{0,1:T(8,128)(2,1)S(1)} %copy-done.1, pred[]{:T(512)S(6)} %eq.8), kind=kLoop, calls=%fused_computation.12 | loop fusion | flops 2097152 | bytes 18874368 | tf_op jit(solution)/shard_map/jit(_where)/select_n | solution.py:39
  426.6 3.8 pad_maximum_fusion
  430.4 9.2 %copy.19 = f32[2048,1024]{1,0:T(8,128)} copy(f32[2048,1024]{0,1:T(8,128)} %pad_maximum_fusion) | data formatting | bytes 16777216 | tf_op jit(solution)/shard_map/concatenate | solution.py:40
  (2 shorter events, 0.0 us)
Async XLA Ops:
  11.3 101.3 %all-to-all-start = ((bf16[32,2048,32]{1,2,0:T(8,128)(2,1)}), bf16[32,2048,32]{1,2,0:T(8,128)(2,1)}, u32[]{:S(2)}, u32[]{:S(2)}) async-start(bf16[32,2048,32]{1,2,0:T(8,128)(2,1)} %bitcast.33), calls=%async_computation | async-start | bytes 8388608 | tf_op jit(solution)/shard_map/all_to_all | solution.py:15
  18.8 234.6 %all-reduce.3.cloned.1.call-start = ((), (), s32[]{:S(2)}) async-start(), calls=%async_computation.1 | async-start | bytes 4194304 | tf_op jit(solution)/shard_map/psum | solution.py:9
  112.6 2.8 copy-start.2
  123.5 285.1 %all-reduce.5.cloned.1.call-start = ((), (), s32[]{:S(2)}) async-start(), calls=%async_computation.2 | async-start | bytes 4194304 | tf_op jit(solution)/shard_map/psum | solution.py:9
  253.3 8.8 %copy-start = (bf16[1024,1024]{0,1:T(8,128)(2,1)S(1)}, bf16[1024,1024]{0,1:T(8,128)(2,1)}, u32[]{:S(2)}) copy-start(bf16[1024,1024]{0,1:T(8,128)(2,1)} %all-reduce.3.cloned.1.call-done) | copy-start | bytes 6291460
  408.5 13.3 %copy-start.1 = (bf16[1024,1024]{0,1:T(8,128)(2,1)S(1)}, bf16[1024,1024]{0,1:T(8,128)(2,1)}, u32[]{:S(2)}) copy-start(bf16[1024,1024]{0,1:T(8,128)(2,1)} %all-reduce.5.cloned.1.call-done) | copy-start | bytes 6291460
Sparse Core Ops, SparseCore 0:
  123.6 129.6 all-reduce.2
  269.0 139.4 all-reduce.4
where the time goes:
time: 447 us; the launch traced here: 446 us
  waiting for transfers between devices  363 us (81%)
  matrix products  25.7 us (6%)
  local copies, waits for them, and re-layouts  19.9 us (4%)
  other arithmetic  16.4 us (4%)
  between operations  13.5 us (3%)
  starting transfers between devices  7.51 us (2%)
    psum x2, waiting for transfers between devices, spread(): return lax.psum(jnp.where(mine, shard, jnp.zeros_like(shard)), axis)  269 us
    all_to_all x1, waiting for transfers between devices, local(): lax.all_to_all(right_sides, ('rows', 'rhs'), split_axis=0, concat_axis=1,...  93.8 us
    dot_general x2, matrix products, local(): jnp.dot(col_panels[panel_id], solved, preferred_element_type=jnp.float32)  22 us
    concatenate x1, local copies, waits for them, and re-layouts, local(): current = jnp.concatenate([top_rows, current[panel_size:]], axis=0)  9.24 us
  transfers between devices with their start and end apart: 3, of which 3 were waited for; matrix products, arithmetic and copies ran while one was open for 0% of the time, Pallas kernels for 0%

commit v1 on v0

--- a/solution.py
+++ b/solution.py
@@ -12,7 +12,16 @@
 def local(right_sides, col_panels, diag_inverses):
     panel_size = diag_inverses.shape[1]
     early_solved = None
-    gathered = lax.all_to_all(right_sides, ("rows", "rhs"), split_axis=0, concat_axis=1, tiled=True)
+    turn_surface = lambda local_array, which_axis: jnp.concatenate(
+        lax.all_to_all(
+            jnp.stack(jnp.split(local_array, lax.axis_size(which_axis), axis=0), axis=0),
+            axis_name=which_axis,
+            split_axis=0,
+            concat_axis=0,
+        ),
+        axis=1,
+    )
+    gathered = turn_surface(right_sides, ("rows", "rhs"))
     current = gathered.astype(jnp.float32)
     rows_dev = current.shape[0]
     panel_count = diag_inverses.shape[0]

time: 447 us -> 493 us (1.10)
  local copies, waits for them, and re-layouts: 19.9 us -> 65.3 us
    unnamed x4 -> x35, local copies, waits for them, and re-layouts: 0.01 us -> 48.6 us
where the time goes in v1:
time: 493 us; the launch traced here: 492 us
  waiting for transfers between devices  363 us (74%)
  local copies, waits for them, and re-layouts  65.3 us (13%)
  matrix products  25.7 us (5%)
  other arithmetic  16.4 us (3%)
  between operations  13.5 us (3%)
  starting transfers between devices  7.51 us (2%)
    psum x2, waiting for transfers between devices, spread(): return lax.psum(jnp.where(mine, shard, jnp.zeros_like(shard)), axis)  269 us
    all_to_all x1, waiting for transfers between devices, local(): lax.all_to_all(jnp.stack(jnp.split(local_array, lax.axis_size(which_axis)...  93.8 us
    unnamed x35, local copies, waits for them, and re-layouts  48.6 us
    dot_general x2, matrix products, local(): jnp.dot(col_panels[panel_id], solved, preferred_element_type=jnp.float32)  22 us
  transfers between devices with their start and end apart: 3, of which 3 were waited for; matrix products, arithmetic and copies ran while one was open for 0% of the time, Pallas kernels for 0%

profile of v1, /device:TPU:0, one launch (start us, length us, event | category | flops | bytes accessed | tf_op | source)
XLA Modules:
  0.0 491.8 jit_solution(14525344205852373317)
XLA Ops:
  6.5 1.6 bitcast_dynamic-update-slice_fusion.31
  8.1 1.6 bitcast_dynamic-update-slice_fusion.30
  9.7 1.6 bitcast_dynamic-update-slice_fusion.29
  11.2 1.6 bitcast_dynamic-update-slice_fusion.28
  12.8 1.6 bitcast_dynamic-update-slice_fusion.27
  14.4 1.6 bitcast_dynamic-update-slice_fusion.26
  15.9 1.6 bitcast_dynamic-update-slice_fusion.25
  17.5 1.6 bitcast_dynamic-update-slice_fusion.24
  19.1 1.6 bitcast_dynamic-update-slice_fusion.23
  20.6 1.6 bitcast_dynamic-update-slice_fusion.22
  22.2 1.6 bitcast_dynamic-update-slice_fusion.21
  23.8 1.6 bitcast_dynamic-update-slice_fusion.20
  25.3 1.6 bitcast_dynamic-update-slice_fusion.19
  26.9 1.6 bitcast_dynamic-update-slice_fusion.18
  28.5 1.6 bitcast_dynamic-update-slice_fusion.17
  30.0 1.6 bitcast_dynamic-update-slice_fusion.16
  31.6 1.6 bitcast_dynamic-update-slice_fusion.15
  33.2 1.6 bitcast_dynamic-update-slice_fusion.14
  34.7 1.6 bitcast_dynamic-update-slice_fusion.13
  36.3 1.6 bitcast_dynamic-update-slice_fusion.12
  37.9 1.6 bitcast_dynamic-update-slice_fusion.11
  39.4 1.6 bitcast_dynamic-update-slice_fusion.10
  41.0 1.6 bitcast_dynamic-update-slice_fusion.9
  42.6 1.6 bitcast_dynamic-update-slice_fusion.8
  44.2 1.6 bitcast_dynamic-update-slice_fusion.7
  45.7 1.6 bitcast_dynamic-update-slice_fusion.6
  47.3 1.6 bitcast_dynamic-update-slice_fusion.5
  48.9 1.6 bitcast_dynamic-update-slice_fusion.4
  50.4 1.6 bitcast_dynamic-update-slice_fusion.3
  52.0 1.6 bitcast_dynamic-update-slice_fusion.2
  53.6 1.6 bitcast_dynamic-update-slice_fusion.1
  55.1 1.6 bitcast_dynamic-update-slice_fusion
  56.7 7.4 %all-to-all-start = ((bf16[32,2048,32]{1,2,0:T(8,128)(2,1)}), bf16[32,2048,32]{1,2,0:T(8,128)(2,1)}, u32[]{:S(2)}, u32[]{:S(2)}) async-start(bf16[32,2048,32]{1,2,0:T(8,128)(2,1)} %bitcast_dynamic-update-slice_fusion), calls=%async_computation | async-start | bytes 8388608 | tf_op jit(solution)/shard_map/all_to_all | solution.py:16
  64.1 0.0 all-reduce.3.cloned.1.call-start
  64.2 93.8 %all-to-all-done = bf16[32,2048,32]{1,2,0:T(8,128)(2,1)} async-done(((bf16[32,2048,32]{1,2,0:T(8,128)(2,1)}), bf16[32,2048,32]{1,2,0:T(8,128)(2,1)}, u32[]{:S(2)}, u32[]{:S(2)}) %all-to-all-start) | async-done | bytes 4194336 | tf_op jit(solution)/shard_map/all_to_all | solution.py:16
  158.0 9.4 %conditional.2 = (bf16[1024,1024]{0,1:T(8,128)(2,1)S(1)}) conditional(s32[]{:T(128)} %convert_element_type.35, () %tuple.18, (bf16[2,1024,1024]{2,1,0:T(8,128)(2,1)}, bf16[2048,32,32]{0,2,1:T(8,128)(2,1)}) %tuple.19), branch_computations={%region_0.0_spmd, %region_1.0_spmd} | conditional | flops 2148532224 | bytes 31457316 | solution.py:37
  158.0 0.0 copy-start.2
  158.0 2.0 slice.38
  160.0 0.9 copy-done.2
  160.8 3.7 fusion.3
  164.5 2.9 copy.47
  167.4 1.5 broadcast_select_fusion
  168.8 0.0 all-reduce.3.cloned.1.call-update
  168.9 0.0 all-reduce.5.cloned.1.call-start
  168.9 129.8 %all-reduce.3.cloned.1.call-done = bf16[1024,1024]{0,1:T(8,128)(2,1)} async-done(((bf16[1024,1024]{0,1:T(8,128)(2,1)}), bf16[1024,1024]{0,1:T(8,128)(2,1)}) %all-reduce.3.cloned.1.call-update) | async-done | bytes 2097168 | tf_op jit(solution)/shard_map/psum | solution.py:9
  298.7 0.0 copy-start
  298.7 8.7 %subtract_select_fusion.1 = f32[2048,1024]{0,1:T(8,128)S(1)} fusion(bf16[2048,1024]{0,1:T(8,128)(2,1)} %bitcast.41, bf16[1024,1024]{0,1:T(8,128)(2,1)} %all-reduce.3.cloned.1.call-done, bf16[2,2048,1024]{2,1,0:T(8,128)(2,1)} %param.8, pred[2048]{0:T(1024)(128)(4,1)S(1)} %fusion.17), kind=kOutput, calls=%fused_computation.9 | convolution fusion | flops 4301258752 | bytes 18876416 | tf_op jit(solution)/shard_map/dot_general | solution.py:45
  307.4 0.0 copy-done
  307.4 4.9 fusion.18
  312.3 0.4 conditional.3
  312.3 0.3 broadcast.22.clone
  312.8 1.5 broadcast_select_fusion.1
  314.2 0.0 all-reduce.5.cloned.1.call-update
  314.3 139.6 %all-reduce.5.cloned.1.call-done = bf16[1024,1024]{0,1:T(8,128)(2,1)} async-done(((bf16[1024,1024]{0,1:T(8,128)(2,1)}), bf16[1024,1024]{0,1:T(8,128)(2,1)}) %all-reduce.5.cloned.1.call-update) | async-done | bytes 2097168 | tf_op jit(solution)/shard_map/psum | solution.py:9
  453.9 0.0 copy-start.1
  453.9 13.3 %subtract_select_fusion = f32[2048,1024]{0,1:T(8,128)} fusion(f32[1024,1024]{0,1:T(8,128)} %get-tuple-element.39, f32[1024,1024]{0,1:T(8,128)} %get-tuple-element.36, bf16[1024,1024]{0,1:T(8,128)(2,1)} %all-reduce.5.cloned.1.call-done, bf16[2,2048,1024]{2,1,0:T(8,128)(2,1)} %param.8, pred[2048]{0:T(1024)(128)(4,1)S(1)} %fusion.16), kind=kOutput, calls=%fused_computation.8 | convolution fusion | flops 4301258752 | bytes 23070720 | tf_op jit(solution)/shard_map/dot_general | solution.py:45
  467.2 0.0 copy-done.1
  467.2 4.7 slice_select_fusion
  471.9 3.8 pad_maximum_fusion
  475.7 9.2 %copy.44 = f32[2048,1024]{1,0:T(8,128)} copy(f32[2048,1024]{0,1:T(8,128)} %pad_maximum_fusion) | data formatting | bytes 16777216 | tf_op jit(solution)/shard_map/concatenate | solution.py:49
  (2 shorter events, 0.0 us)
Async XLA Ops:
  56.7 101.3 %all-to-all-start = ((bf16[32,2048,32]{1,2,0:T(8,128)(2,1)}), bf16[32,2048,32]{1,2,0:T(8,128)(2,1)}, u32[]{:S(2)}, u32[]{:S(2)}) async-start(bf16[32,2048,32]{1,2,0:T(8,128)(2,1)} %bitcast_dynamic-update-slice_fusion), calls=%async_computation | async-start | bytes 8388608 | tf_op jit(solution)/shard_map/all_to_all | solution.py:16
  64.1 234.6 %all-reduce.3.cloned.1.call-start = ((), (), s32[]{:S(2)}) async-start(), calls=%async_computation.1 | async-start | bytes 4194304 | tf_op jit(solution)/shard_map/psum | solution.py:9
  158.0 2.8 copy-start.2
  168.9 285.0 %all-reduce.5.cloned.1.call-start = ((), (), s32[]{:S(2)}) async-start(), calls=%async_computation.2 | async-start | bytes 4194304 | tf_op jit(solution)/shard_map/psum | solution.py:9
  298.7 8.7 %copy-start = (bf16[1024,1024]{0,1:T(8,128)(2,1)S(1)}, bf16[1024,1024]{0,1:T(8,128)(2,1)}, u32[]{:S(2)}) copy-start(bf16[1024,1024]{0,1:T(8,128)(2,1)} %all-reduce.3.cloned.1.call-done) | copy-start | bytes 6291460
  453.9 13.3 %copy-start.1 = (bf16[1024,1024]{0,1:T(8,128)(2,1)S(1)}, bf16[1024,1024]{0,1:T(8,128)(2,1)}, u32[]{:S(2)}) copy-start(bf16[1024,1024]{0,1:T(8,128)(2,1)} %all-reduce.5.cloned.1.call-done) | copy-start | bytes 6291460
Sparse Core Ops, SparseCore 0:
  169.0 129.6 all-reduce.2
  314.4 139.4 all-reduce.4
